TPU v7x, 32 devices: a whole 2x2x4 slice. The times are simulated.
32 devices in a mesh: groups: 2 (over x), spatial: 16 (over z, y, core).
Axes of the slice: x: 2, y: 2, z: 4, core: 2. Of those that a mesh axis runs over, the one named last changes fastest.
Arguments:
- fields: bfloat16 [1024, 128, 768], P(('groups', 'spatial')), parts along dimension 0, may hold values from -6 to 6
- norm1_gain: float32 [768], replicated, may hold values from 0.5 to 1.5
- norm1_bias: float32 [768], replicated, may hold values from -3 to 3
- spectral_w1: float32 [2, 8, 96, 96], replicated, may hold values from -0.4375 to 0.4375
- spectral_b1: float32 [2, 8, 96], replicated, may hold values from -3 to 3
- spectral_w2: float32 [2, 8, 96, 96], replicated, may hold values from -0.4375 to 0.4375
- spectral_b2: float32 [2, 8, 96], replicated, may hold values from -3 to 3
- norm2_gain: float32 [768], replicated, may hold values from 0.5 to 1.5
- norm2_bias: float32 [768], replicated, may hold values from -3 to 3
- fc1_weight: bfloat16 [768, 3072], replicated, may hold values from -0.21875 to 0.21875
- fc1_bias: float32 [3072], replicated, may hold values from -3 to 3
- fc2_weight: bfloat16 [3072, 768], replicated, may hold values from -0.109375 to 0.109375
- fc2_bias: float32 [768], replicated, may hold values from -3 to 3
Outputs:
- next_state: bfloat16 [1024, 128, 768], P(('groups', 'spatial')), parts along dimension 0
- anomaly: bfloat16 [1024, 128, 768], P(('groups', 'spatial')), parts along dimension 0
There are 2 independent parts, one for each index of `groups`. A program takes and returns all parts, laid end to end along the dimension named above; an argument that names none is the same for every part. Nothing has to cross between parts.
All inputs are finite; a program needn't handle non-finite values.
Results may differ from a plain program's by a relative error of at most 0.0056.
Values may be sent and summed in bfloat16 or wider, within the bound.
A program may use at most 192 MiB of HBM per device.

v0:
```python
import math
import jax
import jax.numpy as jnp
from jax import lax
from jax.sharding import Mesh, PartitionSpec as P

MEMBERS = 8
EPSILON = 1e-06
SHRINK = 0.01
FULL_PRECISION = lax.Precision.HIGHEST


def from_behind(block, axis, distance):
    devices = range(lax.axis_size(axis))
    route = [((i - distance) % len(devices), i) for i in devices]
    return lax.ppermute(block, axis, route)


def layer_norm(values, gain, offset_term):
    center = values - jnp.mean(values, axis=-1, keepdims=True)
    spread = jnp.mean(center * center, axis=-1, keepdims=True)
    return center * lax.rsqrt(spread + EPSILON) * gain + offset_term


def soft_shrink(values):
    return jnp.where(
        values > SHRINK, values - SHRINK, jnp.where(values < -SHRINK, values + SHRINK, 0.0)
    )


def contract(form, left, right):
    return jnp.einsum(form, left, right, precision=FULL_PRECISION)


def block_product(values, weight):
    return jnp.einsum("...bi,bio->...bo", values, weight, precision=FULL_PRECISION)


def angle_table(first_len, second_len, modulus):
    first_index = lax.broadcasted_iota(jnp.int32, (first_len, second_len), 0)
    second_index = lax.broadcasted_iota(jnp.int32, (first_len, second_len), 1)
    phase = first_index * second_index % modulus
    return phase.astype(jnp.float32) * (2.0 * math.pi / modulus)


def spectral_layer(real_part, imag_part, w_first, b_first, w_second, b_second):
    shape = real_part.shape
    block_count = w_first.shape[1]
    split_shape = shape[:-1] + (block_count, shape[-1] // block_count)
    real_part = real_part.reshape(split_shape)
    imag_part = imag_part.reshape(split_shape)
    hidden_real = jax.nn.relu(
        block_product(real_part, w_first[0]) - block_product(imag_part, w_first[1]) + b_first[0]
    )
    hidden_imag = jax.nn.relu(
        block_product(imag_part, w_first[0]) + block_product(real_part, w_first[1]) + b_first[1]
    )
    mixed_real = (
        block_product(hidden_real, w_second[0])
        - block_product(hidden_imag, w_second[1])
        + b_second[0]
    )
    mixed_imag = (
        block_product(hidden_imag, w_second[0])
        + block_product(hidden_real, w_second[1])
        + b_second[1]
    )
    return (soft_shrink(mixed_real).reshape(shape), soft_shrink(mixed_imag).reshape(shape))


def longitude_forward(normed, lon_len):
    angles = angle_table(lon_len, lon_len // 2, lon_len)
    factor = 1.0 / math.sqrt(lon_len)
    real_part = contract("rld,lk->rkd", normed, jnp.cos(angles) * factor)
    imag_part = -contract("rld,lk->rkd", normed, jnp.sin(angles) * factor)
    return (real_part, imag_part)


def longitude_inverse(real_part, imag_part, lon_len):
    half_len = lon_len // 2
    angles = angle_table(lon_len, half_len, lon_len)
    column_index = lax.broadcasted_iota(jnp.int32, (1, half_len), 1)
    weights = jnp.where(column_index == 0, 1.0, 2.0) / math.sqrt(lon_len)
    cosine_table = jnp.cos(angles) * weights
    sine_table = jnp.sin(angles) * weights
    return contract("rkd,lk->rld", real_part, cosine_table) - contract(
        "rkd,lk->rld", imag_part, sine_table
    )


def latitude_work(real_part, imag_part, w_first, b_first, w_second, b_second):
    member_rows, mode_count, channels = real_part.shape
    lat_len = member_rows // MEMBERS
    angles = angle_table(lat_len, lat_len, lat_len)
    factor = 1.0 / math.sqrt(lat_len)
    cosine_table = jnp.cos(angles) * factor
    sine_table = jnp.sin(angles) * factor
    grid_real = real_part.reshape(MEMBERS, lat_len, mode_count, channels)
    grid_imag = imag_part.reshape(MEMBERS, lat_len, mode_count, channels)
    spec_real = contract("qp,mpkd->mqkd", cosine_table, grid_real) + contract(
        "qp,mpkd->mqkd", sine_table, grid_imag
    )
    spec_imag = contract("qp,mpkd->mqkd", cosine_table, grid_imag) - contract(
        "qp,mpkd->mqkd", sine_table, grid_real
    )
    mixed_real, mixed_imag = spectral_layer(
        spec_real, spec_imag, w_first, b_first, w_second, b_second
    )
    back_real = contract("qp,mpkd->mqkd", cosine_table, mixed_real) - contract(
        "qp,mpkd->mqkd", sine_table, mixed_imag
    )
    back_imag = contract("qp,mpkd->mqkd", cosine_table, mixed_imag) + contract(
        "qp,mpkd->mqkd", sine_table, mixed_real
    )
    return (
        back_real.reshape(member_rows, mode_count, channels),
        back_imag.reshape(member_rows, mode_count, channels),
    )


def on_device(
    fields,
    norm1_gain,
    norm1_bias,
    spectral_w1,
    spectral_b1,
    spectral_w2,
    spectral_b2,
    norm2_gain,
    norm2_bias,
    fc1_weight,
    fc1_bias,
    fc2_weight,
    fc2_bias,
):
    row_count, lon_len, channels = fields.shape
    state = fields.astype(jnp.float32)
    normed = layer_norm(state, norm1_gain, norm1_bias)
    real_part, imag_part = longitude_forward(normed, lon_len)
    real_part, imag_part = (
        lax.all_to_all(real_part, "spatial", split_axis=1, concat_axis=0, tiled=True),
        lax.all_to_all(imag_part, "spatial", split_axis=1, concat_axis=0, tiled=True),
    )
    real_part, imag_part = latitude_work(
        real_part, imag_part, spectral_w1, spectral_b1, spectral_w2, spectral_b2
    )
    real_part, imag_part = (
        lax.all_to_all(real_part, "spatial", split_axis=0, concat_axis=1, tiled=True),
        lax.all_to_all(imag_part, "spatial", split_axis=0, concat_axis=1, tiled=True),
    )
    filtered = longitude_inverse(real_part, imag_part, lon_len)
    residual = (filtered + normed + state).reshape(row_count * lon_len, channels)
    normed2 = layer_norm(residual, norm2_gain, norm2_bias).astype(jnp.bfloat16)
    hidden = jax.nn.gelu(
        jnp.dot(normed2, fc1_weight, preferred_element_type=jnp.float32) + fc1_bias,
        approximate=False,
    ).astype(jnp.bfloat16)
    updated = residual + jnp.dot(hidden, fc2_weight, preferred_element_type=jnp.float32) + fc2_bias
    next_state = updated.astype(jnp.bfloat16).reshape(row_count, lon_len, channels)
    return next_state


def ensemble_step(next_state):
    state_values = next_state.astype(jnp.float32)
    summed = lax.psum(state_values, "member")
    anomaly = (state_values - summed / MEMBERS).astype(jnp.bfloat16)
    return (next_state, anomaly)


def solution(mesh):
    placed = (
        P(("groups", "spatial"), None, None),
        P(),
        P(),
        P(),
        P(),
        P(),
        P(),
        P(),
        P(),
        P(),
        P(),
        P(),
        P(),
    )
    update = jax.shard_map(
        on_device,
        mesh=mesh,
        in_specs=placed,
        out_specs=P(("groups", "spatial"), None, None),
        check_vma=False,
    )
    member_span = mesh.shape["spatial"] // MEMBERS
    ensemble_mesh = Mesh(
        mesh.devices.reshape(mesh.shape["groups"], MEMBERS, member_span),
        ("groups", "member", "half"),
    )
    member_rows = P(("groups", "member", "half"), None, None)
    spread = jax.shard_map(
        ensemble_step,
        mesh=ensemble_mesh,
        in_specs=(member_rows,),
        out_specs=(member_rows, member_rows),
        check_vma=False,
    )

    def step(*args):
        return spread(update(*args))

    return step
```

profile of v0, /device:TPU:0, one launch (start us, length us, event | category | flops | bytes accessed | tf_op | source)
XLA Modules:
  0.0 1506.0 jit_solution(8603126026089970054)
XLA Ops:
  7.6 9.6 negate_bitcast_fusion
  17.2 6.6 copy.60
  23.8 7.5 all-to-all-start.1
  31.3 12.0 fusion.94
  43.3 6.3 copy.57
  49.6 95.7 %all-to-all-done.1 = f32[32,64,768]{2,0,1:T(8,128)} async-done(((f32[32,64,768]{2,0,1:T(8,128)}), f32[32,64,768]{2,0,1:T(8,128)}, u32[]{:S(2)}, u32[]{:S(2)}) %all-to-all-start.1) | async-done | bytes 6291488 | tf_op jit(solution)/shard_map/all_to_all | solution.py:142
  145.3 28.5 %all-to-all-start = ((f32[32,64,768]{2,0,1:T(8,128)}), f32[32,64,768]{2,0,1:T(8,128)}, u32[]{:S(2)}, u32[]{:S(2)}) async-start(f32[32,64,768]{2,0,1:T(8,128)} %copy.57), calls=%async_computation | async-start | bytes 12582912 | tf_op jit(solution)/shard_map/all_to_all | solution.py:141
  177.4 7.9 fusion.74
  185.3 7.8 fusion.76
  193.1 94.8 %all-to-all-done = f32[32,64,768]{2,0,1:T(8,128)} async-done(((f32[32,64,768]{2,0,1:T(8,128)}), f32[32,64,768]{2,0,1:T(8,128)}, u32[]{:S(2)}, u32[]{:S(2)}) %all-to-all-start) | async-done | bytes 6291488 | tf_op jit(solution)/shard_map/all_to_all | solution.py:141
  294.3 7.9 subtract_bitcast_fusion.1
  302.2 9.9 reshape.102
  312.1 13.7 fusion.58
  325.9 9.9 fusion.60
  335.8 8.2 add_bitcast_fusion.1
  343.9 9.9 reshape.101
  353.8 13.1 add_maximum_fusion
  367.0 9.5 fusion.50
  376.5 9.9 fusion.52
  386.4 9.6 add_maximum_fusion.1
  396.0 14.9 select_bitcast_fusion
  410.9 10.9 copy.70
  421.9 9.6 reshape.104
  431.5 12.2 select_bitcast_fusion.1
  443.7 10.9 copy.69
  454.7 9.6 reshape.103
  464.2 8.3 fusion.128
  472.5 8.7 subtract_bitcast_fusion
  481.8 6.7 copy.72
  488.4 28.2 %all-to-all-start.2 = ((f32[512,4,768]{2,1,0:T(4,128)}), f32[512,4,768]{2,1,0:T(4,128)}, u32[]{:S(2)}, u32[]{:S(2)}) async-start(f32[512,4,768]{2,1,0:T(4,128)} %copy.72), calls=%async_computation.2 | async-start | bytes 12582912 | tf_op jit(solution)/shard_map/all_to_all | solution.py:148
  516.7 8.6 fusion.126
  525.3 6.7 add_bitcast_fusion
  532.5 6.7 copy.76
  539.2 91.6 %all-to-all-done.2 = f32[512,4,768]{2,1,0:T(4,128)} async-done(((f32[512,4,768]{2,1,0:T(4,128)}), f32[512,4,768]{2,1,0:T(4,128)}, u32[]{:S(2)}, u32[]{:S(2)}) %all-to-all-start.2) | async-done | bytes 6291488 | tf_op jit(solution)/shard_map/all_to_all | solution.py:148
  630.7 28.5 %all-to-all-start.3 = ((f32[512,4,768]{2,1,0:T(4,128)}), f32[512,4,768]{2,1,0:T(4,128)}, u32[]{:S(2)}, u32[]{:S(2)}) async-start(f32[512,4,768]{2,1,0:T(4,128)} %copy.76), calls=%async_computation.3 | async-start | bytes 12582912 | tf_op jit(solution)/shard_map/all_to_all | solution.py:149
  659.3 4.0 copy.73
  663.3 6.7 copy.74
  670.0 7.7 all_to_all.57
  677.7 95.6 %all-to-all-done.3 = f32[512,4,768]{2,1,0:T(4,128)} async-done(((f32[512,4,768]{2,1,0:T(4,128)}), f32[512,4,768]{2,1,0:T(4,128)}, u32[]{:S(2)}, u32[]{:S(2)}) %all-to-all-start.3) | async-done | bytes 6291488 | tf_op jit(solution)/shard_map/all_to_all | solution.py:149
  773.3 4.0 copy.77
  777.3 6.7 copy.78
  784.1 7.9 all_to_all.61
  792.0 15.1 %fusion.134 = f32[128,32,768]{2,0,1:T(8,128)} fusion(f32[32,64,768]{2,1,0:T(8,128)} %all_to_all.57, f32[64]{0:T(128)S(1)} %fusion.172), kind=kOutput, calls=%fused_computation.149 | convolution fusion | flops 2416041984 | bytes 18874624 | tf_op jit(solution)/shard_map/rkd,lk->rld/dot_general | solution.py:32
  807.1 19.1 %fusion.262 = (f32[32,128]{1,0:T(8,128)S(1)}, f32[32,128,768]{2,1,0:T(8,128)S(1)}) fusion(f32[768]{0:T(1024)S(1)} %copy-done.16, f32[768]{0:T(1024)S(1)} %copy-done.18, f32[32,128]{1,0:T(8,128)S(1)} %copy-done.12, f32[32,128]{1,0:T(8,128)S(1)} %copy-done.10, bf16[32,128,768]{2,1,0:T(8,128)(2,1)} %param.14, f32[128,32,768]{2,0,1:T(8,128)} %fusion.134, ...), kind=kOutput, calls=%fused_computation.276 | convolution fusion | flops 2444349440 | bytes 37804288 | tf_op jit(solution)/shard_map/rkd,lk->rld/dot_general | solution.py:32
  830.8 126.3 %fusion.2.clone.6 = bf16[4096,3072]{1,0:T(8,128)(2,1)} fusion(bf16[4096,768]{1,0:T(8,128)(2,1)S(1)} %fusion.47, bf16[768,3072]{1,0:T(8,128)(2,1)} %param.23, f32[3072]{0:T(1024)S(1)} %copy-done.21), kind=kOutput, calls=%fused_computation.3.clone.clone.clone.clone.clone.1 | convolution fusion | flops 20157825024 | bytes 36188160 | tf_op jit(solution)/shard_map/dot_general | solution.py:155
  957.2 27.6 %fusion.49 = bf16[4096,768]{1,0:T(8,128)(2,1)} fusion(f32[32,128,768]{2,1,0:T(8,128)} %copy-done, bf16[3072,768]{1,0:T(8,128)(2,1)} %param.25, f32[768]{0:T(1024)S(1)} %copy-done.22, bf16[4096,3072]{1,0:T(8,128)(2,1)} %fusion.2.clone.6), kind=kOutput, calls=%fused_computation.61 | convolution fusion | flops 19336790016 | bytes 48761856 | tf_op jit(solution)/shard_map/dot_general | solution.py:158
  984.7 509.6 %all-reduce.1 = f32[32,128,768]{2,1,0:T(8,128)} all-reduce(bf16[32,128,768]{2,1,0:T(8,128)(2,1)} %bitcast.202), channel_id=1, replica_groups=mesh['groups'=2,'member'=8,'half'=2] {'member'}, use_global_device_ids=true, to_apply=%region_4.6 | all-reduce | flops 3145728 | bytes 18874368 | tf_op jit(solution)/shard_map/psum | solution.py:165
  1494.3 11.2 subtract_convert_fusion
  (91 shorter events, 22.4 us)
Async XLA Ops:
  0.6 4.6 copy-start.3
  0.6 7.0 copy-start.15
  0.7 7.0 copy-start.17
  5.2 26.0 %copy-start.9 = (f32[32,128]{1,0:T(8,128)}, f32[32,128]{1,0:T(8,128)S(1)}, u32[]{:S(2)}) copy-start(f32[32,128]{1,0:T(8,128)S(1)} %broadcast_multiply_fusion.1) | copy-start | bytes 49156
  7.6 23.6 %copy-start.11 = (f32[32,128]{1,0:T(8,128)}, f32[32,128]{1,0:T(8,128)S(1)}, u32[]{:S(2)}) copy-start(f32[32,128]{1,0:T(8,128)S(1)} %add_rsqrt_fusion) | copy-start | bytes 49156
  23.8 121.5 %all-to-all-start.1 = ((f32[32,64,768]{2,0,1:T(8,128)}), f32[32,64,768]{2,0,1:T(8,128)}, u32[]{:S(2)}, u32[]{:S(2)}) async-start(f32[32,64,768]{2,0,1:T(8,128)} %copy.60), calls=%async_computation.1 | async-start | bytes 12582912 | tf_op jit(solution)/shard_map/all_to_all | solution.py:142
  49.6 124.2 %copy-start.13 = (f32[2,8,96]{2,1,0:T(8,128)S(1)}, f32[2,8,96]{2,1,0:T(8,128)}, u32[]{:S(2)}) copy-start(f32[2,8,96]{2,1,0:T(8,128)} %param.18) | copy-start | bytes 18436
  49.6 124.3 %copy-start.14 = (f32[2,8,96]{2,1,0:T(8,128)S(1)}, f32[2,8,96]{2,1,0:T(8,128)}, u32[]{:S(2)}) copy-start(f32[2,8,96]{2,1,0:T(8,128)} %param.20) | copy-start | bytes 18436
  145.3 142.6 %all-to-all-start = ((f32[32,64,768]{2,0,1:T(8,128)}), f32[32,64,768]{2,0,1:T(8,128)}, u32[]{:S(2)}, u32[]{:S(2)}) async-start(f32[32,64,768]{2,0,1:T(8,128)} %copy.57), calls=%async_computation | async-start | bytes 12582912 | tf_op jit(solution)/shard_map/all_to_all | solution.py:141
  193.1 101.2 %slice-start.10 = ((s8[6291456]{0:T(1024)(128)(4,1)}), s8[2097152]{0:T(1024)(128)(4,1)S(1)}, s32[]{:S(2)}) async-start(s8[6291456]{0:T(1024)(128)(4,1)} %bitcast.200), calls=%async_computation.14 | async-start | bytes 4194304
  287.9 6.4 slice-start.11
  291.6 2.7 copy-start.4
  302.2 9.9 copy-start.5
  312.1 13.8 copy-start.1
  312.1 23.6 %slice-start.4 = ((s8[6291456]{0:T(1024)(128)(4,1)}), s8[4194304]{0:T(1024)(128)(4,1)S(1)}, s32[]{:S(2)}) async-start(s8[6291456]{0:T(1024)(128)(4,1)} %bitcast.189), calls=%async_computation.8 | async-start | bytes 8388608
  312.1 23.6 %slice-start.8 = ((s8[6291456]{0:T(1024)(128)(4,1)}), s8[4194304]{0:T(1024)(128)(4,1)S(1)}, s32[]{:S(2)}) async-start(s8[6291456]{0:T(1024)(128)(4,1)} %bitcast.198), calls=%async_computation.12 | async-start | bytes 8388608
  325.9 9.9 slice-start.5
  325.9 9.9 slice-start.9
  353.8 13.2 copy-start.6
  367.0 9.5 copy-start.7
  367.0 19.4 %slice-start = ((s8[8388608]{0:T(1024)(128)(4,1)}), s8[4194304]{0:T(1024)(128)(4,1)S(1)}, s32[]{:S(2)}) async-start(s8[8388608]{0:T(1024)(128)(4,1)} %bitcast.182), calls=%async_computation.4 | async-start | bytes 8388608
  367.0 19.4 %slice-start.6 = ((s8[8388608]{0:T(1024)(128)(4,1)}), s8[4194304]{0:T(1024)(128)(4,1)S(1)}, s32[]{:S(2)}) async-start(s8[8388608]{0:T(1024)(128)(4,1)} %bitcast.192), calls=%async_computation.10 | async-start | bytes 8388608
  376.5 9.9 slice-start.1
  376.5 9.9 slice-start.7
  396.0 14.9 copy-start.2
  421.8 9.6 copy-start.8
  488.4 36.9 %slice-start.2 = ((s8[6291456]{0:T(1024)(128)(4,1)}), s8[2097152]{0:T(1024)(128)(4,1)S(1)}, s32[]{:S(2)}) async-start(s8[6291456]{0:T(1024)(128)(4,1)} %bitcast.184), calls=%async_computation.6 | async-start | bytes 4194304
  488.4 142.3 %all-to-all-start.2 = ((f32[512,4,768]{2,1,0:T(4,128)}), f32[512,4,768]{2,1,0:T(4,128)}, u32[]{:S(2)}, u32[]{:S(2)}) async-start(f32[512,4,768]{2,1,0:T(4,128)} %copy.72), calls=%async_computation.2 | async-start | bytes 12582912 | tf_op jit(solution)/shard_map/all_to_all | solution.py:148
  516.7 8.7 slice-start.3
  630.7 142.6 %all-to-all-start.3 = ((f32[512,4,768]{2,1,0:T(4,128)}), f32[512,4,768]{2,1,0:T(4,128)}, u32[]{:S(2)}, u32[]{:S(2)}) async-start(f32[512,4,768]{2,1,0:T(4,128)} %copy.76), calls=%async_computation.3 | async-start | bytes 12582912 | tf_op jit(solution)/shard_map/all_to_all | solution.py:149
  791.9 15.1 %copy-start.10 = (f32[32,128]{1,0:T(8,128)S(1)}, f32[32,128]{1,0:T(8,128)}, u32[]{:S(2)}) copy-start(f32[32,128]{1,0:T(8,128)} %copy-done.9) | copy-start | bytes 49156
  792.0 15.1 %copy-start.12 = (f32[32,128]{1,0:T(8,128)S(1)}, f32[32,128]{1,0:T(8,128)}, u32[]{:S(2)}) copy-start(f32[32,128]{1,0:T(8,128)} %copy-done.11) | copy-start | bytes 49156
  792.0 15.1 %copy-start.16 = (f32[768]{0:T(1024)S(1)}, f32[768]{0:T(1024)}, u32[]{:S(2)}) copy-start(f32[768]{0:T(1024)} %param.16) | copy-start | bytes 9220
  792.0 15.1 %copy-start.18 = (f32[768]{0:T(1024)S(1)}, f32[768]{0:T(1024)}, u32[]{:S(2)}) copy-start(f32[768]{0:T(1024)} %param.15) | copy-start | bytes 9220
  826.2 4.6 copy-start
  826.2 1.5 copy-start.19
  826.3 1.5 copy-start.20
  827.8 3.0 copy-start.21
  830.8 126.3 %copy-start.22 = (f32[768]{0:T(1024)S(1)}, f32[768]{0:T(1024)}, u32[]{:S(2)}) copy-start(f32[768]{0:T(1024)} %param.26) | copy-start | bytes 9220
where the time goes:
time: 1520 us; the launch traced here: 1510 us
  blocking collectives  510 us (34%)
  waiting for transfers between devices  378 us (25%)
  matrix products  367 us (24%)
  local copies, waits for them, and re-layouts  136 us (9%)
  starting transfers between devices  92.8 us (6%)
  other arithmetic  21.4 us (1%)
    psum x1, blocking collectives, ensemble_step(): summed = lax.psum(state_values, 'member')  510 us
    dot_general x1, matrix products, on_device(): jnp.dot(normed2, fc1_weight, preferred_element_type=jnp.float32) + fc1_bias  126 us
    dot_general x12, matrix products, contract(): return jnp.einsum(form, left, right, precision=FULL_PRECISION)  120 us
    all_to_all x1, waiting for transfers between devices, on_device(): lax.all_to_all(imag_part, 'spatial', split_axis=1, concat_axis=0, tiled=T...  95.7 us
    all_to_all x1, waiting for transfers between devices, on_device(): lax.all_to_all(imag_part, 'spatial', split_axis=0, concat_axis=1, tiled=T...  95.6 us
    all_to_all x1, waiting for transfers between devices, on_device(): lax.all_to_all(real_part, 'spatial', split_axis=1, concat_axis=0, tiled=T...  94.8 us
    dot_general x8, matrix products, block_product(): jnp.einsum('...bi,bio->...bo', values, weight, precision=FULL_PRECISION)  92.8 us
    all_to_all x1, waiting for transfers between devices, on_device(): lax.all_to_all(real_part, 'spatial', split_axis=0, concat_axis=1, tiled=T...  91.6 us
  transfers between devices with their start and end apart: 4, of which 4 were waited for; matrix products, arithmetic and copies ran while one was open for 5% of the time, Pallas kernels for 0%

commit v1 on v0

--- a/solution.py
+++ b/solution.py
@@ -162,7 +162,7 @@
 
 def ensemble_step(next_state):
     state_values = next_state.astype(jnp.float32)
-    summed = lax.psum(state_values, "member")
+    summed = jnp.sum(lax.all_gather(state_values, "member"), axis=0)
     anomaly = (state_values - summed / MEMBERS).astype(jnp.bfloat16)
     return (next_state, anomaly)
 

time: 1520 us -> 2980 us (1.96)
  waiting for transfers between devices: 378 us -> 2300 us
  blocking collectives: 510 us -> 0 us
  other arithmetic: 21.4 us -> 63.5 us
    all_gather x0 -> x1, waiting for transfers between devices: none -> 1920 us  [ensemble_step(): summed = jnp.sum(lax.all_gather(state_values, 'member'), axis=0)]
    psum x1 -> x0, blocking collectives: 510 us -> none  [ensemble_step(): summed = lax.psum(state_values, 'member')]
    reduce_sum x0 -> x1, other arithmetic: none -> 36 us  [ensemble_step(): summed = jnp.sum(lax.all_gather(state_values, 'member'), axis=0)]
  transfers between devices with their start and end apart: 4 -> 5, of which waited for: 4 -> 5; matrix products, arithmetic and copies ran while one was open for 5% -> 2% of each run, Pallas kernels for 0% -> 0%
where the time goes in v1:
time: 2980 us; the launch traced here: 2970 us
  waiting for transfers between devices  2300 us (77%)
  matrix products  366 us (12%)
  local copies, waits for them, and re-layouts  139 us (5%)
  starting transfers between devices  92.8 us (3%)
  other arithmetic  63.5 us (2%)
    all_gather x1, waiting for transfers between devices, ensemble_step(): summed = jnp.sum(lax.all_gather(state_values, 'member'), axis=0)  1920 us
    dot_general x1, matrix products, on_device(): jnp.dot(normed2, fc1_weight, preferred_element_type=jnp.float32) + fc1_bias  126 us
    dot_general x12, matrix products, contract(): return jnp.einsum(form, left, right, precision=FULL_PRECISION)  120 us
    all_to_all x1, waiting for transfers between devices, on_device(): lax.all_to_all(imag_part, 'spatial', split_axis=1, concat_axis=0, tiled=T...  95.7 us
    all_to_all x1, waiting for transfers between devices, on_device(): lax.all_to_all(imag_part, 'spatial', split_axis=0, concat_axis=1, tiled=T...  95.2 us
    all_to_all x1, waiting for transfers between devices, on_device(): lax.all_to_all(real_part, 'spatial', split_axis=1, concat_axis=0, tiled=T...  94.7 us
    dot_general x8, matrix products, block_product(): jnp.einsum('...bi,bio->...bo', values, weight, precision=FULL_PRECISION)  92.7 us
    all_to_all x1, waiting for transfers between devices, on_device(): lax.all_to_all(real_part, 'spatial', split_axis=0, concat_axis=1, tiled=T...  91.5 us
  transfers between devices with their start and end apart: 5, of which 5 were waited for; matrix products, arithmetic and copies ran while one was open for 2% of the time, Pallas kernels for 0%

profile of v1, /device:TPU:0, one launch (start us, length us, event | category | flops | bytes accessed | tf_op | source)
XLA Modules:
  0.0 2972.7 jit_solution(14970059498883837415)
XLA Ops:
  14.2 9.6 negate_bitcast_fusion
  23.8 6.6 copy.60
  30.3 7.5 all-to-all-start.1
  37.8 12.0 fusion.94
  49.8 6.3 copy.57
  56.2 95.7 %all-to-all-done.1 = f32[32,64,768]{2,0,1:T(8,128)} async-done(((f32[32,64,768]{2,0,1:T(8,128)}), f32[32,64,768]{2,0,1:T(8,128)}, u32[]{:S(2)}, u32[]{:S(2)}) %all-to-all-start.1) | async-done | bytes 6291488 | tf_op jit(solution)/shard_map/all_to_all | solution.py:142
  151.9 28.5 all-to-all-start
  184.0 7.9 fusion.74
  191.9 7.9 fusion.76
  199.8 94.7 %all-to-all-done = f32[32,64,768]{2,0,1:T(8,128)} async-done(((f32[32,64,768]{2,0,1:T(8,128)}), f32[32,64,768]{2,0,1:T(8,128)}, u32[]{:S(2)}, u32[]{:S(2)}) %all-to-all-start) | async-done | bytes 6291488 | tf_op jit(solution)/shard_map/all_to_all | solution.py:141
  300.8 7.9 subtract_bitcast_fusion.1
  308.7 9.9 reshape.102
  318.7 13.7 fusion.58
  332.4 9.9 fusion.60
  342.3 8.2 add_bitcast_fusion.1
  350.4 9.9 reshape.101
  360.3 13.1 add_maximum_fusion
  373.5 9.5 fusion.50
  383.0 9.9 fusion.52
  392.9 9.6 add_maximum_fusion.1
  402.5 14.9 select_bitcast_fusion
  417.4 10.9 copy.70
  428.4 9.6 reshape.104
  438.0 12.2 select_bitcast_fusion.1
  450.3 11.0 copy.69
  461.2 9.6 reshape.103
  470.8 8.3 fusion.128
  479.1 8.7 subtract_bitcast_fusion
  488.3 6.6 copy.72
  495.0 28.3 all-to-all-start.2
  523.2 8.6 fusion.126
  531.9 6.7 add_bitcast_fusion
  539.0 6.7 copy.76
  545.7 91.5 %all-to-all-done.2 = f32[512,4,768]{2,1,0:T(4,128)} async-done(((f32[512,4,768]{2,1,0:T(4,128)}), f32[512,4,768]{2,1,0:T(4,128)}, u32[]{:S(2)}, u32[]{:S(2)}) %all-to-all-start.2) | async-done | bytes 6291488 | tf_op jit(solution)/shard_map/all_to_all | solution.py:148
  637.3 28.1 all-to-all-start.3
  669.9 6.7 copy.74
  676.6 7.7 all_to_all.57
  684.3 95.2 %all-to-all-done.3 = f32[512,4,768]{2,1,0:T(4,128)} async-done(((f32[512,4,768]{2,1,0:T(4,128)}), f32[512,4,768]{2,1,0:T(4,128)}, u32[]{:S(2)}, u32[]{:S(2)}) %all-to-all-start.3) | async-done | bytes 6291488 | tf_op jit(solution)/shard_map/all_to_all | solution.py:149
  783.5 6.7 copy.78
  790.2 7.7 all_to_all.61
  798.0 15.2 fusion.134
  813.1 19.3 fusion.262
  837.0 126.3 %fusion.2.clone.6 = bf16[4096,3072]{1,0:T(8,128)(2,1)} fusion(bf16[4096,768]{1,0:T(8,128)(2,1)S(1)} %fusion.47, bf16[768,3072]{1,0:T(8,128)(2,1)} %param.23, f32[3072]{0:T(1024)S(1)} %copy-done.22), kind=kOutput, calls=%fused_computation.3.clone.clone.clone.clone.clone.1 | convolution fusion | flops 20157825024 | bytes 36188160 | tf_op jit(solution)/shard_map/dot_general | solution.py:155
  963.3 26.5 fusion.49
  992.5 6.1 convert_element_type.51
  998.7 1919.6 %all-gather.3.cloned.1.call-done = f32[256,128,768]{2,1,0:T(8,128)} async-done(((f32[32,128,768]{2,1,0:T(8,128)}), f32[256,128,768]{2,1,0:T(8,128)}) %all-gather.3.cloned.1.call-update) | async-done | bytes 100663312 | tf_op jit(solution)/shard_map/all_gather | solution.py:165
  2918.3 36.0 %reduce_sum.49 = f32[32,128,768]{2,1,0:T(8,128)} reduce(f32[8,32,128,768]{3,2,1,0:T(8,128)} %bitcast.61, f32[]{:T(128)} %constant.29.clone.1), dimensions={0}, to_apply=%region_4.6 | reduce | flops 22020096 | bytes 113246208 | tf_op jit(solution)/shard_map/reduce_sum | solution.py:165
  2954.3 11.2 subtract_convert_fusion
  (97 shorter events, 33.6 us)
Async XLA Ops:
  7.2 4.6 copy-start.3
  7.2 7.0 copy-start.16
  7.2 7.0 copy-start.18
  11.8 26.0 copy-start.10
  14.2 23.6 copy-start.12
  30.3 121.5 %all-to-all-start.1 = ((f32[32,64,768]{2,0,1:T(8,128)}), f32[32,64,768]{2,0,1:T(8,128)}, u32[]{:S(2)}, u32[]{:S(2)}) async-start(f32[32,64,768]{2,0,1:T(8,128)} %copy.60), calls=%async_computation.1 | async-start | bytes 12582912 | tf_op jit(solution)/shard_map/all_to_all | solution.py:142
  56.2 124.2 %copy-start.14 = (f32[2,8,96]{2,1,0:T(8,128)S(1)}, f32[2,8,96]{2,1,0:T(8,128)}, u32[]{:S(2)}) copy-start(f32[2,8,96]{2,1,0:T(8,128)} %param.18) | copy-start | bytes 18436
  56.2 124.3 %copy-start.15 = (f32[2,8,96]{2,1,0:T(8,128)S(1)}, f32[2,8,96]{2,1,0:T(8,128)}, u32[]{:S(2)}) copy-start(f32[2,8,96]{2,1,0:T(8,128)} %param.20) | copy-start | bytes 18436
  151.9 142.6 %all-to-all-start = ((f32[32,64,768]{2,0,1:T(8,128)}), f32[32,64,768]{2,0,1:T(8,128)}, u32[]{:S(2)}, u32[]{:S(2)}) async-start(f32[32,64,768]{2,0,1:T(8,128)} %copy.57), calls=%async_computation | async-start | bytes 12582912 | tf_op jit(solution)/shard_map/all_to_all | solution.py:141
  199.8 101.1 %slice-start.10 = ((s8[6291456]{0:T(1024)(128)(4,1)}), s8[2097152]{0:T(1024)(128)(4,1)S(1)}, s32[]{:S(2)}) async-start(s8[6291456]{0:T(1024)(128)(4,1)} %bitcast.201), calls=%async_computation.15 | async-start | bytes 4194304
  294.5 6.4 slice-start.11
  298.1 2.7 copy-start.4
  308.7 9.9 copy-start.6
  318.6 13.7 copy-start.1
  318.6 23.6 slice-start.4
  318.7 23.6 slice-start.8
  332.4 9.9 slice-start.5
  332.4 9.9 slice-start.9
  360.3 13.2 copy-start.7
  373.5 9.5 copy-start.8
  373.5 19.4 slice-start
  373.5 19.4 slice-start.6
  383.0 9.9 slice-start.1
  383.0 9.9 slice-start.7
  402.5 14.9 copy-start.2
  428.4 9.6 copy-start.9
  494.9 36.9 %slice-start.2 = ((s8[6291456]{0:T(1024)(128)(4,1)}), s8[2097152]{0:T(1024)(128)(4,1)S(1)}, s32[]{:S(2)}) async-start(s8[6291456]{0:T(1024)(128)(4,1)} %bitcast.185), calls=%async_computation.7 | async-start | bytes 4194304
  495.0 142.3 %all-to-all-start.2 = ((f32[512,4,768]{2,1,0:T(4,128)}), f32[512,4,768]{2,1,0:T(4,128)}, u32[]{:S(2)}, u32[]{:S(2)}) async-start(f32[512,4,768]{2,1,0:T(4,128)} %copy.72), calls=%async_computation.2 | async-start | bytes 12582912 | tf_op jit(solution)/shard_map/all_to_all | solution.py:148
  523.2 8.6 slice-start.3
  637.3 142.2 %all-to-all-start.3 = ((f32[512,4,768]{2,1,0:T(4,128)}), f32[512,4,768]{2,1,0:T(4,128)}, u32[]{:S(2)}, u32[]{:S(2)}) async-start(f32[512,4,768]{2,1,0:T(4,128)} %copy.76), calls=%async_computation.3 | async-start | bytes 12582912 | tf_op jit(solution)/shard_map/all_to_all | solution.py:149
  665.4 2252.9 %all-gather.3.cloned.1.call-start = ((), (), s32[]{:S(2)}) async-start(), calls=%async_computation.4 | async-start | bytes 113246208 | tf_op jit(solution)/shard_map/all_gather | solution.py:165
  797.9 15.2 copy-start.11
  797.9 15.2 copy-start.13
  798.0 15.2 copy-start.17
  798.0 15.2 copy-start.19
  832.4 4.6 copy-start
  832.5 1.5 copy-start.20
  832.5 1.5 copy-start.21
  834.0 3.0 copy-start.22
  837.0 126.3 %copy-start.23 = (f32[768]{0:T(1024)S(1)}, f32[768]{0:T(1024)}, u32[]{:S(2)}) copy-start(f32[768]{0:T(1024)} %param.26) | copy-start | bytes 9220
  989.8 2.7 copy-start.5
Sparse Core Ops, SparseCore 0:
  998.8 1919.4 all-gather.2
